TPU v7x, 32 devices: a whole 2x2x4 slice. The times are simulated.
32 devices in a mesh: dp: 4 (over y, x), inner: 8 (over z, core).
Axes of the slice: x: 2, y: 2, z: 4, core: 2. Of those that a mesh axis runs over, the one named last changes fastest.
Arguments:
- queries: bfloat16 [32, 32, 128], P(('dp', 'inner'))
- labels: int32 [32], P(('dp', 'inner')), may hold values from 0 to 127
- pages: bfloat16 [128, 1024, 128], P(('dp', 'inner'))
Outputs:
- grad_queries: float32 [32, 32, 128], P(('dp', 'inner'))
- grad_pages: float32 [128, 1024, 128], P(('dp', 'inner'))
All inputs are finite; a program needn't handle non-finite values.
Results may differ from a plain program's by a relative error of at most 0.0029.
Values may be sent and summed in bfloat16 or wider, within the bound.
No kernel may reach another device: no remote copies, remote signals or barrier semaphores. Data moves between devices by JAX's collectives and lax.ppermute only.
A program may use at most 64 MiB of HBM per device.

v0:
```python
import jax
import jax.numpy as jnp
from jax import lax
from jax.sharding import PartitionSpec as P


def shards(queries, labels, pages):
    pages_here, patch_count, width = pages.shape
    token_count = queries.shape[1]
    first_page = lax.axis_index(("dp", "inner")) * pages_here

    def block_terms(query_block, label_block, page_grads):
        rows_count = query_block.shape[0]
        flat_rows = query_block.reshape(rows_count * token_count, width)
        query_grad = jnp.zeros((rows_count * token_count, width), jnp.float32)
        updated = []
        for page_slot in range(pages_here):
            page_block = pages[page_slot]
            scores = lax.dot_general(
                flat_rows, page_block, (((1,), (1,)), ((), ())), preferred_element_type=jnp.float32
            )
            weights = jax.nn.softmax(scores, axis=-1)
            matched = jnp.sum(weights * scores, axis=-1)
            summed = matched.reshape(rows_count, token_count).sum(axis=1)
            signs = jnp.where(
                label_block == first_page + page_slot, jnp.float32(1.0), jnp.float32(-1.0)
            )
            logits = summed - jnp.float32(token_count)
            grad_score = -signs * jax.nn.sigmoid(-signs * logits)
            row_grad = jnp.broadcast_to(grad_score[:, None], (rows_count, token_count)).reshape(
                rows_count * token_count
            )
            dscore = (row_grad[:, None] * weights * (1.0 + scores - matched[:, None])).astype(
                jnp.bfloat16
            )
            query_grad = query_grad + jnp.dot(
                dscore, page_block, preferred_element_type=jnp.float32
            )
            page_term = lax.dot_general(
                dscore, flat_rows, (((0,), (0,)), ((), ())), preferred_element_type=jnp.float32
            )
            updated.append(page_grads[page_slot] + page_term)
        return (query_grad.reshape(rows_count, token_count, width), jnp.stack(updated))

    empty_pages = jnp.zeros((pages_here, patch_count, width), jnp.float32)
    every_query, every_label = (
        lax.all_gather(queries, ("dp", "inner"), axis=0, tiled=True),
        lax.all_gather(labels, ("dp", "inner"), axis=0, tiled=True),
    )
    page_grads = empty_pages
    rows_count = every_query.shape[0]
    query_blocks = every_query.reshape(rows_count // 16, 16, token_count, width)
    label_blocks = every_label.reshape(rows_count // 16, 16)

    def advance(page_carry, inputs):
        block_grad, page_carry = block_terms(inputs[0], inputs[1], page_carry)
        return (page_carry, block_grad)

    page_grads, block_grads = lax.scan(advance, page_grads, (query_blocks, label_blocks))
    grad_buffer = block_grads.reshape(rows_count, token_count, width)
    partial_sum = lax.psum_scatter(
        grad_buffer.astype(jnp.bfloat16), "dp", scatter_dimension=0, tiled=True
    ).astype(jnp.float32)
    grad_queries = lax.psum_scatter(partial_sum, "inner", scatter_dimension=0, tiled=True)
    return (grad_queries, page_grads)


def solution(mesh):
    placed = (P(("dp", "inner"), None, None), P(("dp", "inner")), P(("dp", "inner"), None, None))
    return jax.shard_map(
        shards,
        mesh=mesh,
        in_specs=placed,
        out_specs=(P(("dp", "inner"), None, None), P(("dp", "inner"), None, None)),
        check_vma=False,
    )
```

profile of v0, /device:TPU:0, one launch (start us, length us, event | category | flops | bytes accessed | tf_op | source)
XLA Modules:
  0.0 223.1 jit_solution(10414008605873370452)
XLA Ops:
  8.1 42.0 %all-reduce = s32[32]{0:T(128)S(1)} all-reduce(s32[32]{0:T(128)S(1)} %dynamic-update-slice), channel_id=1, replica_groups=mesh['dp'=4,'inner'=8] {'dp','inner'}, use_global_device_ids=true, to_apply=%add | all-reduce | flops 32 | bytes 256
  50.1 41.4 %all_gather.7 = bf16[32,32,128]{2,1,0:T(8,128)(2,1)S(1)} all-gather(bf16[1,32,128]{2,1,0:T(8,128)(2,1)} %param.5), channel_id=1, replica_groups=mesh['dp'=4,'inner'=8] {'dp','inner'}, dimensions={0}, use_global_device_ids=true | all-gather | bytes 270336 | tf_op jit(solution)/shard_map/all_gather | solution.py:47
  91.6 1.5 broadcast_in_dim.86
  93.0 68.0 %while.15 = (s32[]{:T(128)}, f32[4,1024,128]{2,1,0:T(8,128)}, bf16[2,16,32,128]{3,2,1,0:T(8,128)(2,1)}, s32[2,16]{1,0:T(2,128)S(1)}, s32[]{:T(128)}, /*index=5*/...) while((s32[]{:T(128)}, f32[4,1024,128]{2,1,0:T(8,128)}, ...), condition=%wide.region_17.18_spmd, body=%wide.region_0.17_spmd.sunk | while | flops 1642328576 | bytes 108293800 | solution.py:59
  94.1 0.8 copy-done
  99.6 0.8 copy-done.2
  101.9 2.3 %multiply_convert_fusion.11 = bf16[512,1024]{1,0:T(8,128)(2,1)S(1)} fusion(f32[512,1024]{1,0:T(8,128)} %copy-done.2, f32[512]{0:T(512)S(1)} %multiply_reduce_fusion.9, f32[512]{0:T(512)S(1)} %mul.311, f32[512]{0:T(512)S(1)} %fusion.117, f32[512]{0:T(512)S(1)} %get-tuple-element.248), kind=kLoop, calls=%fused_computation.10.clone.1 | loop fusion | flops 3670016 | bytes 3153920 | tf_op jit(solution)/shard_map/while/body/eval_jaxpr/convert_element_type | solution.py:33
  104.6 2.3 %fusion.125 = f32[1,1024,128]{2,1,0:T(8,128)} fusion(bf16[512,1024]{1,0:T(8,128)(2,1)S(1)} %multiply_convert_fusion.11, bf16[512,128]{1,0:T(8,128)(2,1)S(1)} %bitcast.155, f32[4,1024,128]{2,1,0:T(8,128)} %get-tuple-element.271), kind=kOutput, calls=%fused_computation.25.clone.1 | convolution fusion | flops 134348800 | bytes 2228224 | tf_op jit(solution)/shard_map/while/body/eval_jaxpr/dot_general | solution.py:39
  108.0 0.8 copy-done.1
  110.3 3.2 %multiply_convert_fusion.8 = bf16[512,1024]{1,0:T(8,128)(2,1)} fusion(f32[512,1024]{1,0:T(8,128)} %copy-done.1, f32[512]{0:T(512)S(1)} %multiply_reduce_fusion.8, f32[512]{0:T(512)S(1)} %mul.308, f32[512]{0:T(512)S(1)} %fusion.115, f32[512]{0:T(512)S(1)} %get-tuple-element.246), kind=kLoop, calls=%fused_computation.1.clone.1 | loop fusion | flops 3670016 | bytes 3153920 | tf_op jit(solution)/shard_map/while/body/eval_jaxpr/convert_element_type | solution.py:33
  113.7 2.3 %multiply_convert_fusion.9 = bf16[512,1024]{1,0:T(8,128)(2,1)S(1)} fusion(f32[512,1024]{1,0:T(8,128)} %copy-done, f32[512]{0:T(512)} %copy-done.10, f32[512]{0:T(512)S(1)} %mul.309, f32[512]{0:T(512)} %copy-done.12, f32[512]{0:T(512)S(1)} %get-tuple-element.253), kind=kLoop, calls=%fused_computation.4.clone.1 | loop fusion | flops 3670016 | bytes 3153920 | tf_op jit(solution)/shard_map/while/body/eval_jaxpr/convert_element_type | solution.py:33
  117.3 1.5 multiply_convert_fusion.10
  118.8 1.4 convolution_add_fusion.10
  120.7 1.5 convolution_add_fusion.11
  122.7 1.4 convolution_add_fusion.12
  124.7 1.6 pad_maximum_fusion.2
  126.3 0.7 copy-done.14
  128.1 0.8 copy-done
  133.6 0.8 copy-done.2
  135.9 2.3 %multiply_convert_fusion.11 = bf16[512,1024]{1,0:T(8,128)(2,1)S(1)} fusion(f32[512,1024]{1,0:T(8,128)} %copy-done.2, f32[512]{0:T(512)S(1)} %multiply_reduce_fusion.9, f32[512]{0:T(512)S(1)} %mul.311, f32[512]{0:T(512)S(1)} %fusion.117, f32[512]{0:T(512)S(1)} %get-tuple-element.248), kind=kLoop, calls=%fused_computation.10.clone.1 | loop fusion | flops 3670016 | bytes 3153920 | tf_op jit(solution)/shard_map/while/body/eval_jaxpr/convert_element_type | solution.py:33
  138.6 2.3 %fusion.125 = f32[1,1024,128]{2,1,0:T(8,128)} fusion(bf16[512,1024]{1,0:T(8,128)(2,1)S(1)} %multiply_convert_fusion.11, bf16[512,128]{1,0:T(8,128)(2,1)S(1)} %bitcast.155, f32[4,1024,128]{2,1,0:T(8,128)} %get-tuple-element.271), kind=kOutput, calls=%fused_computation.25.clone.1 | convolution fusion | flops 134348800 | bytes 2228224 | tf_op jit(solution)/shard_map/while/body/eval_jaxpr/dot_general | solution.py:39
  142.0 0.8 copy-done.1
  144.3 3.2 %multiply_convert_fusion.8 = bf16[512,1024]{1,0:T(8,128)(2,1)} fusion(f32[512,1024]{1,0:T(8,128)} %copy-done.1, f32[512]{0:T(512)S(1)} %multiply_reduce_fusion.8, f32[512]{0:T(512)S(1)} %mul.308, f32[512]{0:T(512)S(1)} %fusion.115, f32[512]{0:T(512)S(1)} %get-tuple-element.246), kind=kLoop, calls=%fused_computation.1.clone.1 | loop fusion | flops 3670016 | bytes 3153920 | tf_op jit(solution)/shard_map/while/body/eval_jaxpr/convert_element_type | solution.py:33
  147.7 2.3 %multiply_convert_fusion.9 = bf16[512,1024]{1,0:T(8,128)(2,1)S(1)} fusion(f32[512,1024]{1,0:T(8,128)} %copy-done, f32[512]{0:T(512)} %copy-done.10, f32[512]{0:T(512)S(1)} %mul.309, f32[512]{0:T(512)} %copy-done.12, f32[512]{0:T(512)S(1)} %get-tuple-element.253), kind=kLoop, calls=%fused_computation.4.clone.1 | loop fusion | flops 3670016 | bytes 3153920 | tf_op jit(solution)/shard_map/while/body/eval_jaxpr/convert_element_type | solution.py:33
  151.3 1.5 multiply_convert_fusion.10
  152.8 1.4 convolution_add_fusion.10
  154.7 1.5 convolution_add_fusion.11
  156.7 1.4 convolution_add_fusion.12
  158.7 1.6 pad_maximum_fusion.2
  161.1 21.7 %reduce-scatter.3.cloned.1.call-done = bf16[8,32,128]{2,1,0:T(8,128)(2,1)} async-done(((bf16[32,32,128]{2,1,0:T(8,128)(2,1)}), bf16[8,32,128]{2,1,0:T(8,128)(2,1)}) %reduce-scatter.3.cloned.1.call-update) | async-done | bytes 65552 | tf_op jit(solution)/shard_map/reduce_scatter | solution.py:61
  182.8 1.5 convert_element_type.39
  184.3 31.9 %reduce-scatter.5.cloned.1.call-done = f32[1,32,128]{2,1,0:T(8,128)} async-done(((f32[8,32,128]{2,1,0:T(8,128)}), f32[1,32,128]{2,1,0:T(8,128)}) %reduce-scatter.5.cloned.1.call-update) | async-done | bytes 16400 | tf_op jit(solution)/shard_map/reduce_scatter | solution.py:64
  (151 shorter events, 27.4 us)
Async XLA Ops:
  7.2 85.8 %copy-start.4 = (bf16[4,1024,128]{2,1,0:T(8,128)(2,1)S(1)}, bf16[4,1024,128]{2,1,0:T(8,128)(2,1)}, u32[]{:S(2)}) copy-start(bf16[4,1024,128]{2,1,0:T(8,128)(2,1)} %param.7) | copy-start | bytes 3145732
  7.2 175.6 %reduce-scatter.3.cloned.1.call-start = ((), (), s32[]{:S(2)}) async-start(), calls=%async_computation.2 | async-start | bytes 327680 | tf_op jit(solution)/shard_map/reduce_scatter | solution.py:61
  93.0 8.2 %copy-start.18 = (s32[2,16]{1,0:T(2,128)}, s32[2,16]{1,0:T(2,128)S(1)}, u32[]{:S(2)}) copy-start(s32[2,16]{1,0:T(2,128)S(1)} %get-tuple-element.285) | copy-start | bytes 388 | tf_op jit(solution)/shard_map/while
  93.5 1.4 copy-start
  94.9 1.8 copy-start.12
  95.5 1.7 copy-start.10
  99.1 1.3 copy-start.2
  107.5 2.1 copy-start.15
  107.5 2.1 copy-start.16
  107.5 2.1 copy-start.17
  117.3 2.9 %copy-start.6 = (f32[4,1024,128]{2,1,0:T(8,128)S(1)}, f32[4,1024,128]{2,1,0:T(8,128)}, u32[]{:S(2)}) copy-start(f32[4,1024,128]{2,1,0:T(8,128)} %get-tuple-element.271) | copy-start | bytes 6291460 | tf_op jit(solution)/shard_map/while
  120.7 2.0 copy-start.3
  122.7 1.9 copy-start.7
  124.6 1.6 copy-start.13
  124.7 2.3 %copy-start.5 = (bf16[4,1024,128]{2,1,0:T(8,128)(2,1)S(1)}, bf16[4,1024,128]{2,1,0:T(8,128)(2,1)}, u32[]{:S(2)}) copy-start(bf16[4,1024,128]{2,1,0:T(8,128)(2,1)} %get-tuple-element.308) | copy-start | bytes 3145732 | tf_op jit(solution)/shard_map/while
  124.7 2.3 %copy-start.9 = (bf16[2,16,32,128]{3,2,1,0:T(8,128)(2,1)S(1)}, bf16[2,16,32,128]{3,2,1,0:T(8,128)(2,1)}, u32[]{:S(2)}) copy-start(bf16[2,16,32,128]{3,2,1,0:T(8,128)(2,1)} %copy-done.8) | copy-start | bytes 786436 | tf_op jit(solution)/shard_map/while
  124.7 2.3 %copy-start.19 = (s32[2,16]{1,0:T(2,128)S(1)}, s32[2,16]{1,0:T(2,128)}, u32[]{:S(2)}) copy-start(s32[2,16]{1,0:T(2,128)} %copy-done.18) | copy-start | bytes 388 | tf_op jit(solution)/shard_map/while
  127.0 8.2 %copy-start.18 = (s32[2,16]{1,0:T(2,128)}, s32[2,16]{1,0:T(2,128)S(1)}, u32[]{:S(2)}) copy-start(s32[2,16]{1,0:T(2,128)S(1)} %get-tuple-element.285) | copy-start | bytes 388 | tf_op jit(solution)/shard_map/while
  127.5 1.4 copy-start
  128.9 1.8 copy-start.12
  129.5 1.7 copy-start.10
  141.5 2.1 copy-start.15
  141.5 2.1 copy-start.16
  141.5 2.1 copy-start.17
  151.3 2.9 %copy-start.6 = (f32[4,1024,128]{2,1,0:T(8,128)S(1)}, f32[4,1024,128]{2,1,0:T(8,128)}, u32[]{:S(2)}) copy-start(f32[4,1024,128]{2,1,0:T(8,128)} %get-tuple-element.271) | copy-start | bytes 6291460 | tf_op jit(solution)/shard_map/while
  154.7 2.0 copy-start.3
  156.7 1.9 copy-start.7
  158.6 1.6 copy-start.13
  158.7 2.3 %copy-start.5 = (bf16[4,1024,128]{2,1,0:T(8,128)(2,1)S(1)}, bf16[4,1024,128]{2,1,0:T(8,128)(2,1)}, u32[]{:S(2)}) copy-start(bf16[4,1024,128]{2,1,0:T(8,128)(2,1)} %get-tuple-element.308) | copy-start | bytes 3145732 | tf_op jit(solution)/shard_map/while
  158.7 2.3 %copy-start.9 = (bf16[2,16,32,128]{3,2,1,0:T(8,128)(2,1)S(1)}, bf16[2,16,32,128]{3,2,1,0:T(8,128)(2,1)}, u32[]{:S(2)}) copy-start(bf16[2,16,32,128]{3,2,1,0:T(8,128)(2,1)} %copy-done.8) | copy-start | bytes 786436 | tf_op jit(solution)/shard_map/while
  158.7 2.3 %copy-start.19 = (s32[2,16]{1,0:T(2,128)S(1)}, s32[2,16]{1,0:T(2,128)}, u32[]{:S(2)}) copy-start(s32[2,16]{1,0:T(2,128)} %copy-done.18) | copy-start | bytes 388 | tf_op jit(solution)/shard_map/while
  161.0 55.2 %reduce-scatter.5.cloned.1.call-start = ((), (), s32[]{:S(2)}) async-start(), calls=%async_computation.3 | async-start | bytes 147456 | tf_op jit(solution)/shard_map/reduce_scatter | solution.py:64
  (9 other events, 8.8 us)
Sparse Core Ops, SparseCore 0:
  161.1 21.6 reduce-scatter.2
  185.6 30.5 reduce-scatter.4
where the time goes:
time: 224 us; the launch traced here: 223 us
  blocking collectives  83.4 us (37%)
  waiting for transfers between devices  53.7 us (24%)
  other arithmetic  37.3 us (17%)
  matrix products  21.1 us (9%)
  between operations  14.8 us (7%)
  local copies, waits for them, and re-layouts  12.2 us (5%)
    unnamed x1, blocking collectives  42 us
    all_gather x1, blocking collectives, shards(): lax.all_gather(queries, ('dp', 'inner'), axis=0, tiled=True)  41.4 us
    reduce_scatter x1, waiting for transfers between devices, shards(): lax.psum_scatter(partial_sum, 'inner', scatter_dimension=0, tiled=True)  31.9 us
    reduce_scatter x1, waiting for transfers between devices, shards(): lax.psum_scatter(grad_buffer.astype(jnp.bfloat16), 'dp', scatter_dimensio...  21.7 us
    convert_element_type x8, other arithmetic, block_terms(): (row_grad[:, None] * weights * (1.0 + scores - matched[:, None])).astype(...  18.5 us
    dot_general x8, matrix products, block_terms(): jnp.dot(dscore, page_block, preferred_element_type=jnp.float32)  9.52 us
    dot_general x8, matrix products, block_terms(): lax.dot_general(dscore, flat_rows, (((0,), (0,)), ((), ())), preferred_el...  7.48 us
    while x76, local copies, waits for them, and re-layouts  6.3 us
  transfers between devices with their start and end apart: 2, of which 2 were waited for; matrix products, arithmetic and copies ran while one was open for 0% of the time, Pallas kernels for 0%

commit v1 on v0

--- a/solution.py
+++ b/solution.py
@@ -1,7 +1,32 @@
+import functools
 import jax
 import jax.numpy as jnp
 from jax import lax
 from jax.sharding import PartitionSpec as P
+
+
+def handle_the_teams(mine_x, dev_axis):
+    carry, current_arr, all_values = (
+        lax.axis_size(dev_axis),
+        lax.axis_index(dev_axis),
+        mine_x.shape[0],
+    )
+    oldest, now = (mine_x, 1)
+    while now < carry:
+        oldest = jnp.concatenate(
+            [
+                oldest,
+                lax.ppermute(
+                    oldest, dev_axis, [(dev_i, (dev_i - now) % carry) for dev_i in range(carry)]
+                ),
+            ],
+            0,
+        )
+        now = 2 * now
+    return jnp.roll(oldest, current_arr * all_values, 0)
+
+
+fit_orders = functools.partial(handle_the_teams, dev_axis=("dp", "inner"))
 
 
 def shards(queries, labels, pages):
@@ -44,7 +69,7 @@
 
     empty_pages = jnp.zeros((pages_here, patch_count, width), jnp.float32)
     every_query, every_label = (
-        lax.all_gather(queries, ("dp", "inner"), axis=0, tiled=True),
+        fit_orders(queries),
         lax.all_gather(labels, ("dp", "inner"), axis=0, tiled=True),
     )
     page_grads = empty_pages

time: 224 us -> 210 us (0.938)
  blocking collectives: 83.4 us -> 41.9 us
  waiting for transfers between devices: 53.7 us -> 69.7 us
  starting transfers between devices: 0.08 us -> 8.25 us
    all_gather x1 -> x0, blocking collectives: 41.4 us -> none  [shards(): lax.all_gather(queries, ('dp', 'inner'), axis=0, tiled=True)]
    ppermute x0 -> x5, waiting for transfers between devices: none -> 12.8 us  [handle_the_teams(): lax.ppermute(oldest, dev_axis, [(dev_i, (dev_i - now) % carry) for dev_i...]
    ppermute x0 -> x5, starting transfers between devices: none -> 8.17 us  [handle_the_teams(): lax.ppermute(oldest, dev_axis, [(dev_i, (dev_i - now) % carry) for dev_i...]
    reduce_scatter x1, waiting for transfers between devices: 21.7 us -> 24.9 us  [shards(): lax.psum_scatter(grad_buffer.astype(jnp.bfloat16), 'dp', scatter_dimensio...]
  transfers between devices with their start and end apart: 2 -> 7, of which waited for: 2 -> 6; matrix products, arithmetic and copies ran while one was open for 0% -> 0% of each run, Pallas kernels for 0% -> 0%
where the time goes in v1:
time: 210 us; the launch traced here: 209 us
  waiting for transfers between devices  69.7 us (33%)
  blocking collectives  41.9 us (20%)
  other arithmetic  39.3 us (19%)
  matrix products  21.1 us (10%)
  between operations  14.7 us (7%)
  local copies, waits for them, and re-layouts  13.8 us (7%)
  starting transfers between devices  8.25 us (4%)
    unnamed x1, blocking collectives  41.9 us
    reduce_scatter x1, waiting for transfers between devices, shards(): lax.psum_scatter(partial_sum, 'inner', scatter_dimension=0, tiled=True)  31.9 us
    reduce_scatter x1, waiting for transfers between devices, shards(): lax.psum_scatter(grad_buffer.astype(jnp.bfloat16), 'dp', scatter_dimensio...  24.9 us
    convert_element_type x8, other arithmetic, block_terms(): (row_grad[:, None] * weights * (1.0 + scores - matched[:, None])).astype(...  18.5 us
    ppermute x5, waiting for transfers between devices, handle_the_teams(): lax.ppermute(oldest, dev_axis, [(dev_i, (dev_i - now) % carry) for dev_i...  12.8 us
    dot_general x8, matrix products, block_terms(): jnp.dot(dscore, page_block, preferred_element_type=jnp.float32)  9.52 us
    ppermute x5, starting transfers between devices, handle_the_teams(): lax.ppermute(oldest, dev_axis, [(dev_i, (dev_i - now) % carry) for dev_i...  8.17 us
    dot_general x8, matrix products, block_terms(): lax.dot_general(dscore, flat_rows, (((0,), (0,)), ((), ())), preferred_el...  7.48 us
  transfers between devices with their start and end apart: 7, of which 6 were waited for; matrix products, arithmetic and copies ran while one was open for 0% of the time, Pallas kernels for 0%

profile of v1, /device:TPU:0, one launch (start us, length us, event | category | flops | bytes accessed | tf_op | source)
XLA Modules:
  0.0 209.2 jit_solution(15622140624398550905)
XLA Ops:
  7.2 6.5 %collective-permute-start = (bf16[1,32,128]{2,1,0:T(8,128)(2,1)}, bf16[1,32,128]{2,1,0:T(8,128)(2,1)S(1)}, u32[]{:S(2)}, u32[]{:S(2)}) collective-permute-start(bf16[1,32,128]{2,1,0:T(8,128)(2,1)} %param.5), channel_id=1, source_target_pairs={{0,31},{1,0},{2,1},{3,2},{4,3},{5,4},{6,5},{7,6},{8,7},{9,8},{10,9... | collective-permute-start | bytes 24584 | tf_op jit(solution)/shard_map/ppermute | solution.py:19
  14.4 0.8 collective-permute-done
  16.5 3.2 %collective-permute-done.1 = bf16[2,32,128]{2,1,0:T(8,128)(2,1)S(1)} collective-permute-done((bf16[2,32,128]{2,1,0:T(8,128)(2,1)S(1)}, bf16[2,32,128]{2,1,0:T(8,128)(2,1)S(1)}, u32[]{:S(2)}, u32[]{:S(2)}) %collective-permute-start.1) | collective-permute-done | bytes 16416 | tf_op jit(solution)/shard_map/ppermute | solution.py:19
  20.4 4.8 %collective-permute-done.2 = bf16[4,32,128]{2,1,0:T(8,128)(2,1)S(1)} collective-permute-done((bf16[4,32,128]{2,1,0:T(8,128)(2,1)S(1)}, bf16[4,32,128]{2,1,0:T(8,128)(2,1)S(1)}, u32[]{:S(2)}, u32[]{:S(2)}) %collective-permute-start.2) | collective-permute-done | bytes 32800 | tf_op jit(solution)/shard_map/ppermute | solution.py:19
  26.5 4.0 %collective-permute-done.3 = bf16[8,32,128]{2,1,0:T(8,128)(2,1)S(1)} collective-permute-done((bf16[8,32,128]{2,1,0:T(8,128)(2,1)S(1)}, bf16[8,32,128]{2,1,0:T(8,128)(2,1)S(1)}, u32[]{:S(2)}, u32[]{:S(2)}) %collective-permute-start.3) | collective-permute-done | bytes 65568 | tf_op jit(solution)/shard_map/ppermute | solution.py:19
  31.9 41.9 %all-reduce = s32[32]{0:T(128)S(1)} all-reduce(s32[32]{0:T(128)S(1)} %dynamic-update-slice), channel_id=1, replica_groups=mesh['dp'=4,'inner'=8] {'dp','inner'}, use_global_device_ids=true, to_apply=%add | all-reduce | flops 32 | bytes 256
  74.7 1.5 broadcast_in_dim.86
  76.2 67.8 %while.15 = (s32[]{:T(128)}, f32[4,1024,128]{2,1,0:T(8,128)}, bf16[2,16,32,128]{3,2,1,0:T(8,128)(2,1)}, s32[2,16]{1,0:T(2,128)S(1)}, s32[]{:T(128)}, /*index=5*/...) while((s32[]{:T(128)}, f32[4,1024,128]{2,1,0:T(8,128)}, ...), condition=%wide.region_17.18_spmd, body=%wide.region_0.17_spmd.sunk | while | flops 1642328576 | bytes 108293800 | solution.py:84
  77.2 0.8 copy-done
  82.7 0.8 copy-done.2
  85.1 2.3 %multiply_convert_fusion.11 = bf16[512,1024]{1,0:T(8,128)(2,1)S(1)} fusion(f32[512,1024]{1,0:T(8,128)} %copy-done.2, f32[512]{0:T(512)S(1)} %multiply_reduce_fusion.9, f32[512]{0:T(512)S(1)} %mul.312, f32[512]{0:T(512)S(1)} %fusion.117, f32[512]{0:T(512)S(1)} %get-tuple-element.258), kind=kLoop, calls=%fused_computation.10.clone.1 | loop fusion | flops 3670016 | bytes 3153920 | tf_op jit(solution)/shard_map/while/body/eval_jaxpr/convert_element_type | solution.py:58
  87.8 2.3 %fusion.125 = f32[1,1024,128]{2,1,0:T(8,128)} fusion(bf16[512,1024]{1,0:T(8,128)(2,1)S(1)} %multiply_convert_fusion.11, bf16[512,128]{1,0:T(8,128)(2,1)S(1)} %bitcast.155, f32[4,1024,128]{2,1,0:T(8,128)} %get-tuple-element.281), kind=kOutput, calls=%fused_computation.25.clone.1 | convolution fusion | flops 134348800 | bytes 2228224 | tf_op jit(solution)/shard_map/while/body/eval_jaxpr/dot_general | solution.py:64
  93.4 3.2 %multiply_convert_fusion.8 = bf16[512,1024]{1,0:T(8,128)(2,1)} fusion(f32[512,1024]{1,0:T(8,128)} %copy-done.1, f32[512]{0:T(512)S(1)} %multiply_reduce_fusion.8, f32[512]{0:T(512)S(1)} %mul.309, f32[512]{0:T(512)S(1)} %fusion.115, f32[512]{0:T(512)S(1)} %get-tuple-element.256), kind=kLoop, calls=%fused_computation.1.clone.1 | loop fusion | flops 3670016 | bytes 3153920 | tf_op jit(solution)/shard_map/while/body/eval_jaxpr/convert_element_type | solution.py:58
  96.8 2.3 %multiply_convert_fusion.9 = bf16[512,1024]{1,0:T(8,128)(2,1)S(1)} fusion(f32[512,1024]{1,0:T(8,128)} %copy-done, f32[512]{0:T(512)} %copy-done.10, f32[512]{0:T(512)S(1)} %mul.310, f32[512]{0:T(512)} %copy-done.12, f32[512]{0:T(512)S(1)} %get-tuple-element.263), kind=kLoop, calls=%fused_computation.4.clone.1 | loop fusion | flops 3670016 | bytes 3153920 | tf_op jit(solution)/shard_map/while/body/eval_jaxpr/convert_element_type | solution.py:58
  100.4 1.5 multiply_convert_fusion.10
  101.9 1.4 convolution_add_fusion.10
  103.8 1.5 convolution_add_fusion.11
  105.8 1.4 convolution_add_fusion.12
  107.8 1.6 pad_maximum_fusion.5
  111.1 0.8 copy-done
  119.0 2.3 %multiply_convert_fusion.11 = bf16[512,1024]{1,0:T(8,128)(2,1)S(1)} fusion(f32[512,1024]{1,0:T(8,128)} %copy-done.2, f32[512]{0:T(512)S(1)} %multiply_reduce_fusion.9, f32[512]{0:T(512)S(1)} %mul.312, f32[512]{0:T(512)S(1)} %fusion.117, f32[512]{0:T(512)S(1)} %get-tuple-element.258), kind=kLoop, calls=%fused_computation.10.clone.1 | loop fusion | flops 3670016 | bytes 3153920 | tf_op jit(solution)/shard_map/while/body/eval_jaxpr/convert_element_type | solution.py:58
  121.7 2.3 %fusion.125 = f32[1,1024,128]{2,1,0:T(8,128)} fusion(bf16[512,1024]{1,0:T(8,128)(2,1)S(1)} %multiply_convert_fusion.11, bf16[512,128]{1,0:T(8,128)(2,1)S(1)} %bitcast.155, f32[4,1024,128]{2,1,0:T(8,128)} %get-tuple-element.281), kind=kOutput, calls=%fused_computation.25.clone.1 | convolution fusion | flops 134348800 | bytes 2228224 | tf_op jit(solution)/shard_map/while/body/eval_jaxpr/dot_general | solution.py:64
  127.3 3.2 %multiply_convert_fusion.8 = bf16[512,1024]{1,0:T(8,128)(2,1)} fusion(f32[512,1024]{1,0:T(8,128)} %copy-done.1, f32[512]{0:T(512)S(1)} %multiply_reduce_fusion.8, f32[512]{0:T(512)S(1)} %mul.309, f32[512]{0:T(512)S(1)} %fusion.115, f32[512]{0:T(512)S(1)} %get-tuple-element.256), kind=kLoop, calls=%fused_computation.1.clone.1 | loop fusion | flops 3670016 | bytes 3153920 | tf_op jit(solution)/shard_map/while/body/eval_jaxpr/convert_element_type | solution.py:58
  130.7 2.3 %multiply_convert_fusion.9 = bf16[512,1024]{1,0:T(8,128)(2,1)S(1)} fusion(f32[512,1024]{1,0:T(8,128)} %copy-done, f32[512]{0:T(512)} %copy-done.10, f32[512]{0:T(512)S(1)} %mul.310, f32[512]{0:T(512)} %copy-done.12, f32[512]{0:T(512)S(1)} %get-tuple-element.263), kind=kLoop, calls=%fused_computation.4.clone.1 | loop fusion | flops 3670016 | bytes 3153920 | tf_op jit(solution)/shard_map/while/body/eval_jaxpr/convert_element_type | solution.py:58
  134.3 1.5 multiply_convert_fusion.10
  135.8 1.4 convolution_add_fusion.10
  137.7 1.5 convolution_add_fusion.11
  139.7 1.4 convolution_add_fusion.12
  141.7 1.6 pad_maximum_fusion.5
  144.0 24.9 %reduce-scatter.3.cloned.1.call-done = bf16[8,32,128]{2,1,0:T(8,128)(2,1)} async-done(((bf16[32,32,128]{2,1,0:T(8,128)(2,1)}), bf16[8,32,128]{2,1,0:T(8,128)(2,1)}) %reduce-scatter.3.cloned.1.call-update) | async-done | bytes 65552 | tf_op jit(solution)/shard_map/reduce_scatter | solution.py:86
  169.0 1.5 convert_element_type.39
  170.5 31.9 %reduce-scatter.5.cloned.1.call-done = f32[1,32,128]{2,1,0:T(8,128)} async-done(((f32[8,32,128]{2,1,0:T(8,128)}), f32[1,32,128]{2,1,0:T(8,128)}) %reduce-scatter.5.cloned.1.call-update) | async-done | bytes 16400 | tf_op jit(solution)/shard_map/reduce_scatter | solution.py:89
  (176 shorter events, 35.6 us)
Async XLA Ops:
  7.2 69.0 %copy-start.4 = (bf16[4,1024,128]{2,1,0:T(8,128)(2,1)S(1)}, bf16[4,1024,128]{2,1,0:T(8,128)(2,1)}, u32[]{:S(2)}) copy-start(bf16[4,1024,128]{2,1,0:T(8,128)(2,1)} %param.7) | copy-start | bytes 3145732
  7.2 161.8 %reduce-scatter.3.cloned.1.call-start = ((), (), s32[]{:S(2)}) async-start(), calls=%async_computation.2 | async-start | bytes 327680 | tf_op jit(solution)/shard_map/reduce_scatter | solution.py:86
  7.2 8.0 %collective-permute-start = (bf16[1,32,128]{2,1,0:T(8,128)(2,1)}, bf16[1,32,128]{2,1,0:T(8,128)(2,1)S(1)}, u32[]{:S(2)}, u32[]{:S(2)}) collective-permute-start(bf16[1,32,128]{2,1,0:T(8,128)(2,1)} %param.5), channel_id=1, source_target_pairs={{0,31},{1,0},{2,1},{3,2},{4,3},{5,4},{6,5},{7,6},{8,7},{9,8},{10,9... | collective-permute-start | bytes 24584 | tf_op jit(solution)/shard_map/ppermute | solution.py:19
  16.0 3.7 %collective-permute-start.1 = (bf16[2,32,128]{2,1,0:T(8,128)(2,1)S(1)}, bf16[2,32,128]{2,1,0:T(8,128)(2,1)S(1)}, u32[]{:S(2)}, u32[]{:S(2)}) collective-permute-start(bf16[2,32,128]{2,1,0:T(8,128)(2,1)S(1)} %pad_maximum_fusion.3), channel_id=1, source_target_pairs={{0,30},{1,31},{2,0},{3,1},{4,2},{5,3},{6,4},{7,5},{8,6},{9,7},{10,... | collective-permute-start | bytes 49160 | tf_op jit(solution)/shard_map/ppermute | solution.py:19
  20.4 4.8 %collective-permute-start.2 = (bf16[4,32,128]{2,1,0:T(8,128)(2,1)S(1)}, bf16[4,32,128]{2,1,0:T(8,128)(2,1)S(1)}, u32[]{:S(2)}, u32[]{:S(2)}) collective-permute-start(bf16[4,32,128]{2,1,0:T(8,128)(2,1)S(1)} %pad_maximum_fusion.2), channel_id=1, source_target_pairs={{0,28},{1,29},{2,30},{3,31},{4,0},{5,1},{6,2},{7,3},{8,4},{9,5},{1... | collective-permute-start | bytes 98312 | tf_op jit(solution)/shard_map/ppermute | solution.py:19
  25.9 4.6 %collective-permute-start.3 = (bf16[8,32,128]{2,1,0:T(8,128)(2,1)S(1)}, bf16[8,32,128]{2,1,0:T(8,128)(2,1)S(1)}, u32[]{:S(2)}, u32[]{:S(2)}) collective-permute-start(bf16[8,32,128]{2,1,0:T(8,128)(2,1)S(1)} %pad_maximum_fusion.1), channel_id=1, source_target_pairs={{0,24},{1,25},{2,26},{3,27},{4,28},{5,29},{6,30},{7,31},{8,0},{9,1... | collective-permute-start | bytes 196616 | tf_op jit(solution)/shard_map/ppermute | solution.py:19
  30.5 43.4 %collective-permute-start.4 = (bf16[16,32,128]{2,1,0:T(8,128)(2,1)S(1)}, bf16[16,32,128]{2,1,0:T(8,128)(2,1)S(1)}, u32[]{:S(2)}, u32[]{:S(2)}) collective-permute-start(bf16[16,32,128]{2,1,0:T(8,128)(2,1)S(1)} %get-tuple-element.171), channel_id=1, source_target_pairs={{0,16},{1,17},{2,18},{3,19},{4,20},{5,21},{6,22},{7,23},{8,24},{9,... | collective-permute-start | bytes 393224 | tf_op jit(solution)/shard_map/ppermute | solution.py:19
  76.2 8.2 %copy-start.18 = (s32[2,16]{1,0:T(2,128)}, s32[2,16]{1,0:T(2,128)S(1)}, u32[]{:S(2)}) copy-start(s32[2,16]{1,0:T(2,128)S(1)} %get-tuple-element.295) | copy-start | bytes 388 | tf_op jit(solution)/shard_map/while
  78.1 1.8 copy-start.12
  78.7 1.7 copy-start.10
  90.6 2.1 copy-start.15
  90.7 2.1 copy-start.16
  90.7 2.1 copy-start.17
  100.4 2.9 %copy-start.6 = (f32[4,1024,128]{2,1,0:T(8,128)S(1)}, f32[4,1024,128]{2,1,0:T(8,128)}, u32[]{:S(2)}) copy-start(f32[4,1024,128]{2,1,0:T(8,128)} %get-tuple-element.281) | copy-start | bytes 6291460 | tf_op jit(solution)/shard_map/while
  103.8 2.0 copy-start.3
  105.8 1.9 copy-start.7
  107.7 2.3 %copy-start.5 = (bf16[4,1024,128]{2,1,0:T(8,128)(2,1)S(1)}, bf16[4,1024,128]{2,1,0:T(8,128)(2,1)}, u32[]{:S(2)}) copy-start(bf16[4,1024,128]{2,1,0:T(8,128)(2,1)} %get-tuple-element.318) | copy-start | bytes 3145732 | tf_op jit(solution)/shard_map/while
  107.7 2.3 %copy-start.9 = (bf16[2,16,32,128]{3,2,1,0:T(8,128)(2,1)S(1)}, bf16[2,16,32,128]{3,2,1,0:T(8,128)(2,1)}, u32[]{:S(2)}) copy-start(bf16[2,16,32,128]{3,2,1,0:T(8,128)(2,1)} %copy-done.8) | copy-start | bytes 786436 | tf_op jit(solution)/shard_map/while
  107.7 2.3 %copy-start.19 = (s32[2,16]{1,0:T(2,128)S(1)}, s32[2,16]{1,0:T(2,128)}, u32[]{:S(2)}) copy-start(s32[2,16]{1,0:T(2,128)} %copy-done.18) | copy-start | bytes 388 | tf_op jit(solution)/shard_map/while
  110.1 8.2 %copy-start.18 = (s32[2,16]{1,0:T(2,128)}, s32[2,16]{1,0:T(2,128)S(1)}, u32[]{:S(2)}) copy-start(s32[2,16]{1,0:T(2,128)S(1)} %get-tuple-element.295) | copy-start | bytes 388 | tf_op jit(solution)/shard_map/while
  112.0 1.8 copy-start.12
  112.6 1.7 copy-start.10
  124.6 2.1 copy-start.15
  124.6 2.1 copy-start.16
  124.6 2.1 copy-start.17
  134.3 2.9 %copy-start.6 = (f32[4,1024,128]{2,1,0:T(8,128)S(1)}, f32[4,1024,128]{2,1,0:T(8,128)}, u32[]{:S(2)}) copy-start(f32[4,1024,128]{2,1,0:T(8,128)} %get-tuple-element.281) | copy-start | bytes 6291460 | tf_op jit(solution)/shard_map/while
  137.7 2.0 copy-start.3
  139.7 1.9 copy-start.7
  141.6 2.3 %copy-start.5 = (bf16[4,1024,128]{2,1,0:T(8,128)(2,1)S(1)}, bf16[4,1024,128]{2,1,0:T(8,128)(2,1)}, u32[]{:S(2)}) copy-start(bf16[4,1024,128]{2,1,0:T(8,128)(2,1)} %get-tuple-element.318) | copy-start | bytes 3145732 | tf_op jit(solution)/shard_map/while
  141.6 2.3 %copy-start.9 = (bf16[2,16,32,128]{3,2,1,0:T(8,128)(2,1)S(1)}, bf16[2,16,32,128]{3,2,1,0:T(8,128)(2,1)}, u32[]{:S(2)}) copy-start(bf16[2,16,32,128]{3,2,1,0:T(8,128)(2,1)} %copy-done.8) | copy-start | bytes 786436 | tf_op jit(solution)/shard_map/while
  141.7 2.3 %copy-start.19 = (s32[2,16]{1,0:T(2,128)S(1)}, s32[2,16]{1,0:T(2,128)}, u32[]{:S(2)}) copy-start(s32[2,16]{1,0:T(2,128)} %copy-done.18) | copy-start | bytes 388 | tf_op jit(solution)/shard_map/while
  144.0 58.4 %reduce-scatter.5.cloned.1.call-start = ((), (), s32[]{:S(2)}) async-start(), calls=%async_computation.3 | async-start | bytes 147456 | tf_op jit(solution)/shard_map/reduce_scatter | solution.py:89
  (14 other events, 16.0 us)
Sparse Core Ops, SparseCore 0:
  144.1 24.7 reduce-scatter.2
  171.8 30.5 reduce-scatter.4
